TPU v7x, 32 devices: a whole 2x2x4 slice. The times are simulated.
32 devices in a mesh: groups: 2 (over x), row: 16 (over z, y, core).
Axes of the slice: x: 2, y: 2, z: 4, core: 2. Of those that a mesh axis runs over, the one named last changes fastest.
Arguments:
- homolog_embedding: bfloat16 [128, 256, 64], P('groups', 'row'), parts along dimension 0, may hold values from -6 to 6
- pair_state_tiles: bfloat16 [512, 256, 128], P(('groups', 'row')), parts along dimension 0, may hold values from -6 to 6
- alignment_mask: int32 [128, 256], P('groups', 'row'), parts along dimension 0, may hold values 0 or 1
- token_real_mask: int32 [512], P('groups'), parts along dimension 0, may hold values 0 or 1
- lineup_standardize_scaling: float32 [64], replicated, may hold values from 0.1 to 1.9
- former_factor_proj: bfloat16 [64, 32], replicated, may hold values from -0.75 to 0.75
- latter_factor_proj: bfloat16 [64, 32], replicated, may hold values from -0.75 to 0.75
- outer_output_weight: bfloat16 [1024, 128], replicated, may hold values from -0.1875 to 0.1875
- pair_norm_gain: float32 [128], replicated, may hold values from 0.1 to 1.9
- pair_logit_weight: float32 [128, 8], replicated
- content_vector_proj: bfloat16 [64, 256], replicated, may hold values from -0.75 to 0.75
- sigmoid_switch_proj: bfloat16 [64, 256], replicated, may hold values from -0.75 to 0.75
- final_result_proj: bfloat16 [256, 64], replicated, may hold values from -0.375 to 0.375
Outputs:
- alignment_updated: bfloat16 [128, 256, 64], P('groups', 'row'), parts along dimension 0
- pair_updated: bfloat16 [512, 256, 128], P(('groups', 'row')), parts along dimension 0
There are 2 independent parts, one for each index of `groups`. A program takes and returns all parts, laid end to end along the dimension named above; an argument that names none is the same for every part. Nothing has to cross between parts.
All inputs are finite; a program needn't handle non-finite values. No bound on the sum of `alignment_mask` on one device may be relied on, other than what follows from the above.
Results may differ from a plain program's by a relative error of at most 0.007.
Values may be sent and summed in bfloat16 or wider, within the bound.
No kernel may reach another device: no remote copies, remote signals or barrier semaphores. Data moves between devices by JAX's collectives and lax.ppermute only.
A program may use at most 128 MiB of HBM per device.

v0:
```python
import jax
import jax.numpy as jnp
from jax import lax
from jax.sharding import PartitionSpec as P


def layer_normalize(inputs, gain):
    inputs = inputs.astype(jnp.float32)
    center = jnp.mean(inputs, axis=-1, keepdims=True)
    spread = jnp.mean((inputs - center) ** 2, axis=-1, keepdims=True)
    return (inputs - center) * lax.rsqrt(spread + 1e-05) * gain


def pair_terms(folded, local_mask, right_piece, mask_piece):
    product = jnp.einsum("seiz,sje->ijz", folded, right_piece, preferred_element_type=jnp.float32)
    counts = jnp.einsum("si,sj->ij", local_mask, mask_piece, preferred_element_type=jnp.float32)
    return product / (1.0 + counts)[:, :, None]


def shards(
    homolog_embedding,
    pair_state_tiles,
    alignment_mask,
    token_real_mask,
    lineup_standardize_scaling,
    former_factor_proj,
    latter_factor_proj,
    outer_output_weight,
    pair_norm_gain,
    pair_logit_weight,
    content_vector_proj,
    sigmoid_switch_proj,
    final_result_proj,
):
    normed_input = layer_normalize(homolog_embedding, lineup_standardize_scaling).astype(
        jnp.bfloat16
    )
    mask_halved = alignment_mask.astype(jnp.bfloat16)
    mask_float = mask_halved.astype(jnp.float32)
    left_rows = (
        jnp.dot(normed_input, former_factor_proj, preferred_element_type=jnp.float32)
        * mask_float[:, :, None]
    ).astype(jnp.bfloat16)
    factor = former_factor_proj.shape[1]
    channels = outer_output_weight.shape[1]
    weight_cube = outer_output_weight.reshape(factor, factor, channels)
    folded = jnp.einsum(
        "sic,cez->seiz", left_rows, weight_cube, preferred_element_type=jnp.float32
    ).astype(jnp.bfloat16)
    head_count = pair_logit_weight.shape[1]
    head_width = content_vector_proj.shape[1] // head_count
    gathered, gathered_mask = (
        lax.all_gather(normed_input, "row", axis=1, tiled=True),
        lax.all_gather(mask_halved, "row", axis=1, tiled=True),
    )
    right_all = (
        jnp.dot(gathered, latter_factor_proj, preferred_element_type=jnp.float32)
        * gathered_mask.astype(jnp.float32)[:, :, None]
    ).astype(jnp.bfloat16)
    update = pair_terms(folded, mask_halved, right_all, gathered_mask)
    pair_updated = (pair_state_tiles.astype(jnp.float32) + update).astype(jnp.bfloat16)
    pair_normed = layer_normalize(pair_updated, pair_norm_gain)
    logits = jnp.einsum(
        "ijc,ch->hij", pair_normed, pair_logit_weight, precision=lax.Precision.HIGHEST
    )
    logits = jnp.where(token_real_mask[None, None, :] == 1, logits, -1000000000.0)
    weights = jax.nn.softmax(logits, axis=2).astype(jnp.bfloat16)
    seq_count, local_tokens = (normed_input.shape[0], normed_input.shape[1])
    values_all = jnp.dot(gathered, content_vector_proj, preferred_element_type=jnp.float32).astype(
        jnp.bfloat16
    )
    span = values_all.shape[1]
    heads_piece = values_all.reshape(seq_count, span, head_count, head_width)
    term = jnp.einsum("hij,sjhc->sihc", weights, heads_piece, preferred_element_type=jnp.float32)
    average = term.reshape(seq_count, local_tokens, head_count * head_width)
    gate_vals = jax.nn.sigmoid(
        jnp.dot(normed_input, sigmoid_switch_proj, preferred_element_type=jnp.float32)
    )
    gated_output = (gate_vals * average).astype(jnp.bfloat16)
    update_alignment = jnp.dot(gated_output, final_result_proj, preferred_element_type=jnp.float32)
    alignment_updated = (homolog_embedding.astype(jnp.float32) + update_alignment).astype(
        jnp.bfloat16
    )
    return (alignment_updated, pair_updated)


def solution(mesh):
    placed = (
        P("groups", "row", None),
        P(("groups", "row"), None, None),
        P("groups", "row"),
        P("groups"),
        P(),
        P(),
        P(),
        P(),
        P(),
        P(),
        P(),
        P(),
        P(),
    )
    return jax.shard_map(
        shards,
        mesh=mesh,
        in_specs=placed,
        out_specs=(P("groups", "row", None), P(("groups", "row"), None, None)),
        check_vma=False,
    )
```

profile of v0, /device:TPU:0, one launch (start us, length us, event | category | flops | bytes accessed | tf_op | source)
XLA Modules:
  0.0 111.5 jit_solution(13931650329398912923)
XLA Ops:
  7.2 0.0 copy-start
  7.2 0.0 copy-start.3
  7.2 0.0 all-gather.2.cloned.1.call-start
  7.2 1.2 %convert_reduce_fusion.1 = f32[64,16]{1,0:T(8,128)S(1)} fusion(bf16[64,16,64]{2,1,0:T(8,128)(2,1)} %param.13), kind=kLoop, calls=%fused_computation.44 | loop fusion | flops 130048 | bytes 135168 | tf_op jit(solution)/shard_map/reduce_sum | solution.py:9
  8.4 1.3 %fusion.44 = f32[64,16]{1,0:T(8,128)S(1)} fusion(bf16[64,16,64]{2,1,0:T(8,128)(2,1)} %param.13, f32[64,16]{1,0:T(8,128)S(1)} %broadcast_multiply_fusion), kind=kLoop, calls=%fused_computation.47 | loop fusion | flops 261120 | bytes 139264 | tf_op jit(solution)/shard_map/reduce_sum | solution.py:10
  9.8 2.0 %fusion.46 = bf16[64,16,64]{2,1,0:T(8,128)(2,1)} fusion(bf16[64,16,64]{2,1,0:T(8,128)(2,1)} %param.13, f32[64]{0:T(128)} %param.17, f32[64,16]{1,0:T(8,128)S(1)} %add_rsqrt_fusion, f32[64,16]{1,0:T(8,128)S(1)} %broadcast_multiply_fusion), kind=kLoop, calls=%fused_computation.49 | loop fusion | flops 327680 | bytes 270592 | tf_op jit(solution)/shard_map/convert_element_type | solution.py:35
  11.8 0.0 all-gather.2.cloned.1.call-update
  11.8 0.7 fusion.62
  12.5 23.4 %all_gather.7 = bf16[64,256]{0,1:T(8,128)(2,1)S(1)} all-gather(bf16[64,16]{0,1:T(8,128)(2,1)S(1)} %get-tuple-element.11), channel_id=1, replica_groups=mesh['groups'=2,'row'=16] {'row'}, dimensions={1}, use_global_device_ids=true | all-gather | bytes 34816 | tf_op jit(solution)/shard_map/all_gather | solution.py:54
  35.9 0.1 copy.47
  36.0 1.5 %copy.46 = bf16[16,256,128]{1,2,0:T(8,128)(2,1)S(1)} copy(bf16[16,256,128]{2,1,0:T(8,128)(2,1)} %param.14) | data formatting | bytes 2097152 | tf_op args[1]
  37.5 0.7 broadcast_compare_fusion
  38.2 0.1 convolution_add_fusion.1
  38.3 0.0 copy-done.3
  38.3 0.0 copy-start.5
  38.3 6.0 %convert_bitcast_fusion = bf16[64,32,16,128]{3,0,1,2:T(8,128)(2,1)} fusion(bf16[32,32,128]{2,1,0:T(8,128)(2,1)S(1)} %bitcast.59, bf16[64,16,64]{2,1,0:T(8,128)(2,1)} %fusion.46, f32[64,16]{0,1:T(8,128)S(1)} %get-tuple-element.10, bf16[64,32]{0,1:T(8,128)(2,1)} %param.18), kind=kOutput, calls=%fused_computation.6 | convolution fusion | flops 276889600 | bytes 8790016 | tf_op jit(solution)/shard_map/sic,cez->seiz/dot_general | solution.py:47
  44.3 22.9 %all-gather.2.cloned.1.call-done = bf16[64,256,64]{2,1,0:T(8,128)(2,1)} async-done(((bf16[64,16,64]{2,1,0:T(8,128)(2,1)}), bf16[64,256,64]{2,1,0:T(8,128)(2,1)}) %all-gather.2.cloned.1.call-update) | async-done | bytes 2097168 | tf_op jit(solution)/shard_map/all_gather | solution.py:53
  67.2 0.0 copy-done.5
  67.2 3.7 %fusion.19 = bf16[64,256,32,1]{1,2,0,3:T(8,128)(2,1)S(1)} fusion(bf16[64,256,64]{2,1,0:T(8,128)(2,1)} %all-gather.2.cloned.1.call-done, f32[64,256]{1,0:T(8,128)S(1)} %convert_element_type.54, bf16[64,32]{0,1:T(8,128)(2,1)S(1)} %copy-done.5), kind=kOutput, calls=%fused_computation.20 | convolution fusion | flops 68157440 | bytes 3215360 | tf_op jit(solution)/shard_map/dot_general | solution.py:57
  70.9 0.0 copy-start.7
  70.9 0.0 copy-start.8
  70.9 11.0 %convert_reduce_fusion = (f32[16,256]{1,0:T(8,128)S(1)}, bf16[16,256,128]{1,2,0:T(8,128)(2,1)S(1)}) fusion(f32[16,256]{1,0:T(8,128)S(1)} %convolution_add_fusion.1, bf16[64,256,32,1]{1,2,0,3:T(8,128)(2,1)S(1)} %fusion.19, bf16[64,32,16,128]{3,0,1,2:T(8,128)(2,1)} %convert_bitcast_fusion, bf16[16,256,128]{1,2,0:T(8,128)(2,1)S(1)} %copy.46), kind=kOutput, calls=%fused_computation.9 | convolution fusion | flops 2150625280 | bytes 11567104 | tf_op jit(solution)/shard_map/seiz,sje->ijz/dot_general | solution.py:15
  82.0 1.3 %copy.57 = bf16[16,256,128]{2,1,0:T(8,128)(2,1)} copy(bf16[16,256,128]{1,2,0:T(8,128)(2,1)S(1)} %get-tuple-element.13) | data formatting | bytes 2097152
  83.3 0.3 fusion.11
  83.6 0.0 copy-done.7
  83.6 0.0 copy-done.8
  83.7 1.5 %fusion.34 = f32[8,16,256]{2,0,1:T(8,128)S(1)} fusion(bf16[16,256,128]{1,2,0:T(8,128)(2,1)S(1)} %get-tuple-element.13, f32[128]{0:T(128)S(1)} %copy-done.8, f32[16,256]{1,0:T(8,128)S(1)} %add_rsqrt_fusion.1, f32[16,256]{1,0:T(8,128)S(1)} %broadcast_multiply_fusion.1, pred[256]{0:T(512)(128)(4,1)S(1)} %broadcast_compare_fusion, f32[128,8]{0,1:T(8,128)S(1)} %copy-done.7), kind=kOutput, calls=%fused_computation.36 | convolution fusion | flops 52461568 | bytes 1217280 | tf_op jit(solution)/shard_map/ijc,ch->hij/dot_general | solution.py:63
  85.1 0.2 fusion.38
  85.3 0.0 copy-done
  85.3 4.5 %convolution_convert_fusion = bf16[64,256,256]{1,2,0:T(8,128)(2,1)S(1)} fusion(bf16[64,256,64]{2,1,0:T(8,128)(2,1)} %all-gather.2.cloned.1.call-done, bf16[64,256]{1,0:T(8,128)(2,1)S(1)} %copy-done), kind=kOutput, calls=%fused_computation.7 | convolution fusion | flops 541065216 | bytes 10518528 | tf_op jit(solution)/shard_map/dot_general | solution.py:69
  89.9 7.5 %fusion.8 = f32[64,16,8,32]{3,1,0,2:T(8,128)} fusion(bf16[64,256,8,32]{1,3,2,0:T(8,128)(2,1)S(1)} %bitcast.57, bf16[8,16,256,1]{2,0,1,3:T(8,128)(2,1)S(1)} %fusion.38), kind=kOutput, calls=%fused_computation.12 | convolution fusion | flops 134217728 | bytes 9502720 | tf_op jit(solution)/shard_map/hij,sjhc->sihc/dot_general | solution.py:74
  97.4 0.0 copy-start.2
  97.4 0.0 copy-start.6
  97.4 2.9 %copy.54 = f32[64,16,8,32]{0,3,2,1:T(8,128)S(1)} copy(f32[64,16,8,32]{3,1,0,2:T(8,128)} %fusion.8) | data formatting | bytes 2097152 | tf_op jit(solution)/shard_map/hij,sjhc->sihc/transpose | solution.py:74
  100.3 0.0 copy-start.1
  100.3 0.0 copy-start.4
  100.3 1.6 %copy.55 = f32[64,16,256]{2,0,1:T(8,128)} copy(f32[64,16,256]{0,2,1:T(8,128)S(1)} %bitcast.58) | data formatting | bytes 2097152 | tf_op jit(solution)/shard_map/reshape | solution.py:75
  101.9 0.0 copy-done.2
  101.9 0.0 copy-done.6
  101.9 1.6 %fusion.24 = bf16[64,16,256]{2,0,1:T(8,128)(2,1)S(1)} fusion(f32[64,16,256]{2,0,1:T(8,128)} %copy.55, bf16[64,16,64]{2,1,0:T(8,128)(2,1)S(1)} %copy-done.2, bf16[64,256]{1,0:T(8,128)(2,1)S(1)} %copy-done.6), kind=kOutput, calls=%fused_computation.26 | convolution fusion | flops 34865152 | bytes 1736704 | tf_op jit(solution)/shard_map/dot_general | solution.py:77
  103.5 0.0 copy-done.1
  103.6 0.0 copy-done.4
  103.6 1.1 %fusion.25 = bf16[64,16,64]{2,1,0:T(8,128)(2,1)} fusion(bf16[64,16,64]{2,1,0:T(8,128)(2,1)S(1)} %copy-done.1, bf16[64,16,256]{2,0,1:T(8,128)(2,1)S(1)} %fusion.24, bf16[256,64]{0,1:T(8,128)(2,1)S(1)} %copy-done.4), kind=kOutput, calls=%fused_computation.28 | convolution fusion | flops 33751040 | bytes 819200 | tf_op jit(solution)/shard_map/dot_general | solution.py:80
  (5 shorter events, 0.0 us)
Async XLA Ops:
  7.2 78.2 %copy-start = (bf16[64,256]{1,0:T(8,128)(2,1)S(1)}, bf16[64,256]{1,0:T(8,128)(2,1)}, u32[]{:S(2)}) copy-start(bf16[64,256]{1,0:T(8,128)(2,1)} %param.23) | copy-start | bytes 98308
  7.2 31.1 %copy-start.3 = (bf16[1024,128]{1,0:T(8,128)(2,1)S(1)}, bf16[1024,128]{1,0:T(8,128)(2,1)}, u32[]{:S(2)}) copy-start(bf16[1024,128]{1,0:T(8,128)(2,1)} %param.20) | copy-start | bytes 786436
  7.2 60.0 %all-gather.2.cloned.1.call-start = ((), (), s32[]{:S(2)}) async-start(), calls=%async_computation | async-start | bytes 4456448 | tf_op jit(solution)/shard_map/all_gather | solution.py:53
  38.3 28.9 %copy-start.5 = (bf16[64,32]{0,1:T(8,128)(2,1)S(1)}, bf16[64,32]{0,1:T(8,128)(2,1)}, u32[]{:S(2)}) copy-start(bf16[64,32]{0,1:T(8,128)(2,1)} %param.19) | copy-start | bytes 12292
  70.9 12.7 %copy-start.7 = (f32[128,8]{0,1:T(8,128)S(1)}, f32[128,8]{0,1:T(8,128)}, u32[]{:S(2)}) copy-start(f32[128,8]{0,1:T(8,128)} %param.22) | copy-start | bytes 12292
  70.9 12.7 %copy-start.8 = (f32[128]{0:T(128)S(1)}, f32[128]{0:T(128)}, u32[]{:S(2)}) copy-start(f32[128]{0:T(128)} %param.21) | copy-start | bytes 1540
  97.4 4.5 %copy-start.2 = (bf16[64,16,64]{2,1,0:T(8,128)(2,1)S(1)}, bf16[64,16,64]{2,1,0:T(8,128)(2,1)}, u32[]{:S(2)}) copy-start(bf16[64,16,64]{2,1,0:T(8,128)(2,1)} %fusion.46) | copy-start | bytes 393220
  97.4 4.5 %copy-start.6 = (bf16[64,256]{1,0:T(8,128)(2,1)S(1)}, bf16[64,256]{1,0:T(8,128)(2,1)}, u32[]{:S(2)}) copy-start(bf16[64,256]{1,0:T(8,128)(2,1)} %param.24) | copy-start | bytes 98308
  100.3 3.3 %copy-start.1 = (bf16[64,16,64]{2,1,0:T(8,128)(2,1)S(1)}, bf16[64,16,64]{2,1,0:T(8,128)(2,1)}, u32[]{:S(2)}) copy-start(bf16[64,16,64]{2,1,0:T(8,128)(2,1)} %param.13) | copy-start | bytes 393220
  100.3 3.3 %copy-start.4 = (bf16[256,64]{0,1:T(8,128)(2,1)S(1)}, bf16[256,64]{0,1:T(8,128)(2,1)}, u32[]{:S(2)}) copy-start(bf16[256,64]{0,1:T(8,128)(2,1)} %param.25) | copy-start | bytes 98308
Sparse Core Ops, SparseCore 0:
  11.9 55.2 all-gather.1
where the time goes:
time: 112 us
  matrix products  37.2 us (33%)
  blocking collectives  23.4 us (21%)
  waiting for transfers between devices  22.9 us (20%)
  between operations  14.2 us (13%)
  local copies, waits for them, and re-layouts  7.38 us (7%)
  other arithmetic  6.42 us (6%)
    all_gather x1, blocking collectives, shards(): lax.all_gather(mask_halved, 'row', axis=1, tiled=True)  23.4 us
    all_gather x1, waiting for transfers between devices, shards(): lax.all_gather(normed_input, 'row', axis=1, tiled=True)  22.9 us
    dot_general x1, matrix products, pair_terms(): jnp.einsum('seiz,sje->ijz', folded, right_piece, preferred_element_type=j...  11 us
    dot_general x1, matrix products, shards(): jnp.einsum('hij,sjhc->sihc', weights, heads_piece, preferred_element_type...  7.5 us
    dot_general x1, matrix products, shards(): jnp.einsum('sic,cez->seiz', left_rows, weight_cube, preferred_element_typ...  5.96 us
    dot_general x1, matrix products, shards(): jnp.dot(gathered, content_vector_proj, preferred_element_type=jnp.float32)  4.55 us
    dot_general x1, matrix products, shards(): jnp.dot(gathered, latter_factor_proj, preferred_element_type=jnp.float32)  3.72 us
    transpose x1, local copies, waits for them, and re-layouts, shards(): jnp.einsum('hij,sjhc->sihc', weights, heads_piece, preferred_element_type...  2.87 us
  transfers between devices with their start and end apart: 1, of which 1 were waited for; matrix products, arithmetic and copies ran while one was open for 8% of the time, Pallas kernels for 0%

commit v1 on v0

--- a/solution.py
+++ b/solution.py
@@ -51,7 +51,7 @@
     head_width = content_vector_proj.shape[1] // head_count
     gathered, gathered_mask = (
         lax.all_gather(normed_input, "row", axis=1, tiled=True),
-        lax.all_gather(mask_halved, "row", axis=1, tiled=True),
+        jnp.concatenate(lax.all_gather(mask_halved, "row"), axis=1),
     )
     right_all = (
         jnp.dot(gathered, latter_factor_proj, preferred_element_type=jnp.float32)

time: 112 us -> 112 us (level)
  transfers between devices with their start and end apart: 1 -> 1, of which waited for: 1 -> 1; matrix products, arithmetic and copies ran while one was open for 8% -> 9% of each run, Pallas kernels for 0% -> 0%
where the time goes in v1:
time: 112 us
  matrix products  37.9 us (34%)
  blocking collectives  23.4 us (21%)
  waiting for transfers between devices  22.2 us (20%)
  between operations  14.2 us (13%)
  local copies, waits for them, and re-layouts  7.38 us (7%)
  other arithmetic  6.42 us (6%)
    all_gather x1, blocking collectives, shards(): lax.all_gather(mask_halved, 'row')  23.4 us
    all_gather x1, waiting for transfers between devices, shards(): lax.all_gather(normed_input, 'row', axis=1, tiled=True)  22.2 us
    dot_general x1, matrix products, pair_terms(): jnp.einsum('seiz,sje->ijz', folded, right_piece, preferred_element_type=j...  11 us
    dot_general x1, matrix products, shards(): jnp.einsum('hij,sjhc->sihc', weights, heads_piece, preferred_element_type...  7.5 us
    dot_general x1, matrix products, shards(): jnp.einsum('sic,cez->seiz', left_rows, weight_cube, preferred_element_typ...  5.96 us
    dot_general x1, matrix products, shards(): jnp.dot(gathered, content_vector_proj, preferred_element_type=jnp.float32)  4.55 us
    dot_general x1, matrix products, shards(): jnp.dot(gathered, latter_factor_proj, preferred_element_type=jnp.float32)  3.72 us
    transpose x1, local copies, waits for them, and re-layouts, shards(): jnp.einsum('hij,sjhc->sihc', weights, heads_piece, preferred_element_type...  2.87 us
  transfers between devices with their start and end apart: 1, of which 1 were waited for; matrix products, arithmetic and copies ran while one was open for 9% of the time, Pallas kernels for 0%

profile of v1, /device:TPU:0, one launch (start us, length us, event | category | flops | bytes accessed | tf_op | source)
XLA Modules:
  0.0 111.5 jit_solution(1900197976817647296)
XLA Ops:
  7.2 0.0 copy-start
  7.2 0.0 copy-start.3
  7.2 0.0 all-gather.4.cloned.1.call-start
  7.2 1.2 %convert_reduce_fusion.1 = f32[64,16]{1,0:T(8,128)S(1)} fusion(bf16[64,16,64]{2,1,0:T(8,128)(2,1)} %param.13), kind=kLoop, calls=%fused_computation.44 | loop fusion | flops 130048 | bytes 135168 | tf_op jit(solution)/shard_map/reduce_sum | solution.py:9
  8.4 1.3 %fusion.44 = f32[64,16]{1,0:T(8,128)S(1)} fusion(bf16[64,16,64]{2,1,0:T(8,128)(2,1)} %param.13, f32[64,16]{1,0:T(8,128)S(1)} %broadcast_multiply_fusion), kind=kLoop, calls=%fused_computation.47 | loop fusion | flops 261120 | bytes 139264 | tf_op jit(solution)/shard_map/reduce_sum | solution.py:10
  9.8 2.0 %fusion.46 = bf16[64,16,64]{2,1,0:T(8,128)(2,1)} fusion(bf16[64,16,64]{2,1,0:T(8,128)(2,1)} %param.13, f32[64]{0:T(128)} %param.17, f32[64,16]{1,0:T(8,128)S(1)} %add_rsqrt_fusion, f32[64,16]{1,0:T(8,128)S(1)} %broadcast_multiply_fusion), kind=kLoop, calls=%fused_computation.49 | loop fusion | flops 327680 | bytes 270592 | tf_op jit(solution)/shard_map/convert_element_type | solution.py:35
  11.8 0.0 all-gather.4.cloned.1.call-update
  11.8 0.7 convert_convert_fusion
  12.5 23.4 %all-gather.1 = bf16[16,64,16]{1,2,0:T(8,128)(2,1)S(1)} all-gather(bf16[1,64,16]{1,2,0:T(8,128)(2,1)S(1)} %get-tuple-element.9), channel_id=2, replica_groups=mesh['groups'=2,'row'=16] {'row'}, dimensions={0}, use_global_device_ids=true | all-gather | bytes 34816 | tf_op jit(solution)/shard_map/all_gather | solution.py:54
  35.9 0.1 copy.33
  36.0 1.5 %copy.32 = bf16[16,256,128]{1,2,0:T(8,128)(2,1)S(1)} copy(bf16[16,256,128]{2,1,0:T(8,128)(2,1)} %param.14) | data formatting | bytes 2097152 | tf_op args[1]
  37.5 0.7 broadcast_compare_fusion
  38.2 0.8 convolution_add_fusion.1
  39.0 0.0 copy-done.3
  39.0 0.0 copy-start.5
  39.0 6.0 %convert_bitcast_fusion = bf16[64,32,16,128]{3,0,1,2:T(8,128)(2,1)} fusion(bf16[32,32,128]{2,1,0:T(8,128)(2,1)S(1)} %bitcast.65, bf16[64,16,64]{2,1,0:T(8,128)(2,1)} %fusion.46, f32[64,16]{0,1:T(8,128)S(1)} %get-tuple-element.8, bf16[64,32]{0,1:T(8,128)(2,1)} %param.18), kind=kOutput, calls=%fused_computation.6 | convolution fusion | flops 276889600 | bytes 8790016 | tf_op jit(solution)/shard_map/sic,cez->seiz/dot_general | solution.py:47
  45.0 22.2 %all-gather.4.cloned.1.call-done = bf16[64,256,64]{2,1,0:T(8,128)(2,1)} async-done(((bf16[64,16,64]{2,1,0:T(8,128)(2,1)}), bf16[64,256,64]{2,1,0:T(8,128)(2,1)}) %all-gather.4.cloned.1.call-update) | async-done | bytes 2097168 | tf_op jit(solution)/shard_map/all_gather | solution.py:53
  67.2 0.0 copy-done.5
  67.2 3.7 %fusion.19 = bf16[64,256,32,1]{1,2,0,3:T(8,128)(2,1)S(1)} fusion(bf16[64,256,64]{2,1,0:T(8,128)(2,1)} %all-gather.4.cloned.1.call-done, f32[64,256]{1,0:T(8,128)S(1)} %convert_element_type.58, bf16[64,32]{0,1:T(8,128)(2,1)S(1)} %copy-done.5), kind=kOutput, calls=%fused_computation.20 | convolution fusion | flops 68157440 | bytes 3215360 | tf_op jit(solution)/shard_map/dot_general | solution.py:57
  70.9 0.0 copy-start.7
  70.9 0.0 copy-start.8
  70.9 11.0 %convert_reduce_fusion = (f32[16,256]{1,0:T(8,128)S(1)}, bf16[16,256,128]{1,2,0:T(8,128)(2,1)S(1)}) fusion(f32[16,256]{1,0:T(8,128)S(1)} %convolution_add_fusion.1, bf16[64,256,32,1]{1,2,0,3:T(8,128)(2,1)S(1)} %fusion.19, bf16[64,32,16,128]{3,0,1,2:T(8,128)(2,1)} %convert_bitcast_fusion, bf16[16,256,128]{1,2,0:T(8,128)(2,1)S(1)} %copy.32), kind=kOutput, calls=%fused_computation.9 | convolution fusion | flops 2150625280 | bytes 11567104 | tf_op jit(solution)/shard_map/seiz,sje->ijz/dot_general | solution.py:15
  82.0 1.3 %copy.43 = bf16[16,256,128]{2,1,0:T(8,128)(2,1)} copy(bf16[16,256,128]{1,2,0:T(8,128)(2,1)S(1)} %get-tuple-element.11) | data formatting | bytes 2097152
  83.3 0.3 fusion.11
  83.6 0.0 copy-done.7
  83.7 0.0 copy-done.8
  83.7 1.5 %fusion.34 = f32[8,16,256]{2,0,1:T(8,128)S(1)} fusion(bf16[16,256,128]{1,2,0:T(8,128)(2,1)S(1)} %get-tuple-element.11, f32[128]{0:T(128)S(1)} %copy-done.8, f32[16,256]{1,0:T(8,128)S(1)} %add_rsqrt_fusion.1, f32[16,256]{1,0:T(8,128)S(1)} %broadcast_multiply_fusion.1, pred[256]{0:T(512)(128)(4,1)S(1)} %broadcast_compare_fusion, f32[128,8]{0,1:T(8,128)S(1)} %copy-done.7), kind=kOutput, calls=%fused_computation.36 | convolution fusion | flops 52461568 | bytes 1217280 | tf_op jit(solution)/shard_map/ijc,ch->hij/dot_general | solution.py:63
  85.1 0.2 fusion.38
  85.3 0.0 copy-done
  85.3 4.6 %convolution_convert_fusion = bf16[64,256,256]{1,2,0:T(8,128)(2,1)S(1)} fusion(bf16[64,256,64]{2,1,0:T(8,128)(2,1)} %all-gather.4.cloned.1.call-done, bf16[64,256]{1,0:T(8,128)(2,1)S(1)} %copy-done), kind=kOutput, calls=%fused_computation.7 | convolution fusion | flops 541065216 | bytes 10518528 | tf_op jit(solution)/shard_map/dot_general | solution.py:69
  89.9 7.5 %fusion.8 = f32[64,16,8,32]{3,1,0,2:T(8,128)} fusion(bf16[64,256,8,32]{1,3,2,0:T(8,128)(2,1)S(1)} %bitcast.61, bf16[8,16,256,1]{2,0,1,3:T(8,128)(2,1)S(1)} %fusion.38), kind=kOutput, calls=%fused_computation.12 | convolution fusion | flops 134217728 | bytes 9502720 | tf_op jit(solution)/shard_map/hij,sjhc->sihc/dot_general | solution.py:74
  97.4 0.0 copy-start.2
  97.4 0.0 copy-start.6
  97.4 2.9 %copy.40 = f32[64,16,8,32]{0,3,2,1:T(8,128)S(1)} copy(f32[64,16,8,32]{3,1,0,2:T(8,128)} %fusion.8) | data formatting | bytes 2097152 | tf_op jit(solution)/shard_map/hij,sjhc->sihc/transpose | solution.py:74
  100.3 0.0 copy-start.1
  100.3 0.0 copy-start.4
  100.3 1.6 %copy.41 = f32[64,16,256]{2,0,1:T(8,128)} copy(f32[64,16,256]{0,2,1:T(8,128)S(1)} %bitcast.62) | data formatting | bytes 2097152 | tf_op jit(solution)/shard_map/reshape | solution.py:75
  101.9 0.0 copy-done.2
  101.9 0.0 copy-done.6
  101.9 1.6 %fusion.24 = bf16[64,16,256]{2,0,1:T(8,128)(2,1)S(1)} fusion(f32[64,16,256]{2,0,1:T(8,128)} %copy.41, bf16[64,16,64]{2,1,0:T(8,128)(2,1)S(1)} %copy-done.2, bf16[64,256]{1,0:T(8,128)(2,1)S(1)} %copy-done.6), kind=kOutput, calls=%fused_computation.26 | convolution fusion | flops 34865152 | bytes 1736704 | tf_op jit(solution)/shard_map/dot_general | solution.py:77
  103.5 0.0 copy-done.1
  103.6 0.0 copy-done.4
  103.6 1.1 %fusion.25 = bf16[64,16,64]{2,1,0:T(8,128)(2,1)} fusion(bf16[64,16,64]{2,1,0:T(8,128)(2,1)S(1)} %copy-done.1, bf16[64,16,256]{2,0,1:T(8,128)(2,1)S(1)} %fusion.24, bf16[256,64]{0,1:T(8,128)(2,1)S(1)} %copy-done.4), kind=kOutput, calls=%fused_computation.28 | convolution fusion | flops 33751040 | bytes 819200 | tf_op jit(solution)/shard_map/dot_general | solution.py:80
  (5 shorter events, 0.0 us)
Async XLA Ops:
  7.2 78.2 %copy-start = (bf16[64,256]{1,0:T(8,128)(2,1)S(1)}, bf16[64,256]{1,0:T(8,128)(2,1)}, u32[]{:S(2)}) copy-start(bf16[64,256]{1,0:T(8,128)(2,1)} %param.23) | copy-start | bytes 98308
  7.2 31.8 %copy-start.3 = (bf16[1024,128]{1,0:T(8,128)(2,1)S(1)}, bf16[1024,128]{1,0:T(8,128)(2,1)}, u32[]{:S(2)}) copy-start(bf16[1024,128]{1,0:T(8,128)(2,1)} %param.20) | copy-start | bytes 786436
  7.2 60.0 %all-gather.4.cloned.1.call-start = ((), (), s32[]{:S(2)}) async-start(), calls=%async_computation | async-start | bytes 4456448 | tf_op jit(solution)/shard_map/all_gather | solution.py:53
  39.0 28.2 %copy-start.5 = (bf16[64,32]{0,1:T(8,128)(2,1)S(1)}, bf16[64,32]{0,1:T(8,128)(2,1)}, u32[]{:S(2)}) copy-start(bf16[64,32]{0,1:T(8,128)(2,1)} %param.19) | copy-start | bytes 12292
  70.9 12.7 %copy-start.7 = (f32[128,8]{0,1:T(8,128)S(1)}, f32[128,8]{0,1:T(8,128)}, u32[]{:S(2)}) copy-start(f32[128,8]{0,1:T(8,128)} %param.22) | copy-start | bytes 12292
  70.9 12.7 %copy-start.8 = (f32[128]{0:T(128)S(1)}, f32[128]{0:T(128)}, u32[]{:S(2)}) copy-start(f32[128]{0:T(128)} %param.21) | copy-start | bytes 1540
  97.4 4.5 %copy-start.2 = (bf16[64,16,64]{2,1,0:T(8,128)(2,1)S(1)}, bf16[64,16,64]{2,1,0:T(8,128)(2,1)}, u32[]{:S(2)}) copy-start(bf16[64,16,64]{2,1,0:T(8,128)(2,1)} %fusion.46) | copy-start | bytes 393220
  97.4 4.5 %copy-start.6 = (bf16[64,256]{1,0:T(8,128)(2,1)S(1)}, bf16[64,256]{1,0:T(8,128)(2,1)}, u32[]{:S(2)}) copy-start(bf16[64,256]{1,0:T(8,128)(2,1)} %param.24) | copy-start | bytes 98308
  100.3 3.3 %copy-start.1 = (bf16[64,16,64]{2,1,0:T(8,128)(2,1)S(1)}, bf16[64,16,64]{2,1,0:T(8,128)(2,1)}, u32[]{:S(2)}) copy-start(bf16[64,16,64]{2,1,0:T(8,128)(2,1)} %param.13) | copy-start | bytes 393220
  100.3 3.3 %copy-start.4 = (bf16[256,64]{0,1:T(8,128)(2,1)S(1)}, bf16[256,64]{0,1:T(8,128)(2,1)}, u32[]{:S(2)}) copy-start(bf16[256,64]{0,1:T(8,128)(2,1)} %param.25) | copy-start | bytes 98308
Sparse Core Ops, SparseCore 0:
  11.9 55.2 all-gather.3
